TPU v7x, 512 devices: a whole 4x8x8 slice. The times are simulated.
512 devices in a mesh: blade: 256 (over z, y, x), inst: 2 (over core).
Axes of the slice: x: 4, y: 8, z: 8, core: 2. Of those that a mesh axis runs over, the one named last changes fastest.
Arguments:
- tangent_seed: float32 [256, 5, 24, 1024], P('blade', None, 'inst'), may hold values from -6 to 6
- adjoint_seed: float32 [256, 5, 24, 1024], P('blade', None, 'inst'), may hold values from -6 to 6
- jacobian: bfloat16 [256, 24, 25, 1024], P('blade', 'inst'), may hold values from -1 to 4
- precond: bfloat16 [256, 24, 25, 1024], P('blade', 'inst'), may hold values from -1 to 4
- upwind: float32 [256, 1024], P('blade'), may hold values from 0.2 to 1
- up_weight: float32 [256, 256], P('blade'), may hold values from 0.3 to 1.2
- bottom_face_strength: float32 [256, 256], P('blade'), may hold values from 0.3 to 1.2
- up_cells: int32 [256], replicated, may hold values from 0 to 1023, as said below
- lo_cells: int32 [256], replicated, may hold values from 0 to 1023, as said below
- phase_index: int32 [11], replicated, may hold values from 0 to 255
Outputs:
- tangent_out: float32 [256, 5, 24, 1024], P('blade', None, 'inst')
- adjoint_out: float32 [256, 5, 24, 1024], P('blade', None, 'inst')
Inputs may be any that keep to these rules, and one draw needn't show every extreme that they name: `up_cells`: entry f of the table is one of the cells 4 f to 4 f + 3. `lo_cells`: entry f of the table is one of the cells 4 f to 4 f + 3.
All inputs are finite; a program needn't handle non-finite values.
Results may differ from a plain program's by a relative error of at most 0.0003.
Values sent between devices are 32-bit elements; how exact they have to be, the bound alone decides.
No kernel may reach another device: no remote copies, remote signals or barrier semaphores. Data moves between devices by JAX's collectives and lax.ppermute only.
A program may use at most 64 MiB of HBM per device.

v0:
```python
import jax
import jax.numpy as jnp
from jax import lax
from jax.sharding import PartitionSpec as P

SNAPSHOT_COUNT = 24
NH = 11
OMEGA = 0.15


def passed_along(block, axis, distance):
    devices = range(lax.axis_size(axis))
    route = [((i - distance) % len(devices), i) for i in devices]
    return lax.ppermute(block, axis, route)


def spectral(phase_index, passages):
    sampled_moments = jnp.arange(SNAPSHOT_COUNT, dtype=jnp.int32)
    snapshot_displacement = sampled_moments[:, None] - sampled_moments[None, :]
    orders = jnp.arange(1, NH + 1, dtype=jnp.int32)
    wrapped = (
        jnp.mod(orders[:, None, None] * snapshot_displacement[None, :, :], SNAPSHOT_COUNT).astype(
            jnp.float32
        )
        / SNAPSHOT_COUNT
    )
    weights = orders.astype(jnp.float32)[:, None, None]
    skewed = -(2.0 / SNAPSHOT_COUNT) * jnp.sum(weights * jnp.sin(2.0 * jnp.pi * wrapped), axis=0)
    derivative = 0.5 * skewed - 0.5 * skewed.T
    phase_angle = phase_index.astype(jnp.float32)[:, None, None] / passages
    parity = 1.0 - 2.0 * jnp.mod(snapshot_displacement, 2).astype(jnp.float32)
    rotation = (1.0 + parity) / SNAPSHOT_COUNT + 2.0 / SNAPSHOT_COUNT * jnp.sum(
        jnp.cos(2.0 * jnp.pi * (wrapped - phase_angle)), axis=0
    )
    return (derivative, rotation)


def block_apply(blocks, vector):
    variables = vector.shape[1]
    result_rows = []
    for row_index in range(variables):
        summed = blocks[:, :, row_index * variables, :] * vector[:, 0]
        for column_index in range(1, variables):
            summed = (
                summed
                + blocks[:, :, row_index * variables + column_index, :] * vector[:, column_index]
            )
        result_rows.append(summed)
    return jnp.stack(result_rows, axis=1)


def block_apply_t(blocks, vector):
    variables = vector.shape[1]
    result_rows = []
    for column_index in range(variables):
        summed = blocks[:, :, column_index, :] * vector[:, 0]
        for row_index in range(1, variables):
            summed = (
                summed
                + blocks[:, :, row_index * variables + column_index, :] * vector[:, row_index]
            )
        result_rows.append(summed)
    return jnp.stack(result_rows, axis=1)


def instance_mix(matrix, vector):
    return jnp.einsum("ts,pvsc->pvtc", matrix, vector, precision=lax.Precision.HIGHEST)


def cell_mask(cells_table):
    face_count = cells_table.shape[0]
    within = cells_table - 4 * jnp.arange(face_count, dtype=jnp.int32)
    spread = jnp.repeat(within, 4)
    slot_in_group = jnp.mod(jnp.arange(4 * face_count, dtype=jnp.int32), 4)
    return (spread == slot_in_group).astype(jnp.float32)


def face_pick(vector, mask):
    lead = vector.shape[:-1]
    picked = (vector * mask).reshape(lead + (vector.shape[-1] // 4, 4))
    return jnp.sum(picked, axis=-1)


def face_spread(values, mask):
    return jnp.repeat(values, 4, axis=-1) * mask


def regroup(vector, lo_mask, up_mask, derivative, rotation):
    lo_face = face_pick(vector, lo_mask)
    up_face = face_pick(vector, up_mask)
    own_count = vector.shape[2]
    first_row = lax.axis_index("inst") * own_count
    own_deriv = lax.dynamic_slice_in_dim(derivative, first_row, own_count, 0)
    own_rot = lax.dynamic_slice_in_dim(rotation, first_row, own_count, 0)
    own_rot_t = lax.dynamic_slice_in_dim(rotation.T, first_row, own_count, 0)
    return (
        instance_mix(own_deriv, lax.all_gather(vector, "inst", axis=2, tiled=True)),
        instance_mix(own_rot, lax.all_gather(lo_face, "inst", axis=2, tiled=True)),
        instance_mix(own_rot_t, lax.all_gather(up_face, "inst", axis=2, tiled=True)),
    )


def cycle_faces(next_source, previous_source_term):
    from_next = jnp.concatenate([next_source[1:], passed_along(next_source, "blade", -1)], axis=0)
    from_prev = jnp.concatenate(
        [passed_along(previous_source_term, "blade", 1), previous_source_term[:-1]], axis=0
    )
    return (from_next, from_prev)


def on_device(
    tangent_seed,
    adjoint_seed,
    jacobian,
    precond,
    upwind,
    up_weight,
    bottom_face_strength,
    up_cells,
    lo_cells,
    phase_index,
):
    passages = tangent_seed.shape[0] * lax.axis_size("blade")
    derivative, rotation = spectral(phase_index, passages)
    up_mask = cell_mask(up_cells)
    lo_mask = cell_mask(lo_cells)
    dual_field = block_apply_t(precond, adjoint_seed)
    negated = -dual_field
    up_scale = up_weight[:, None, None, :]
    lo_scale = bottom_face_strength[:, None, None, :]
    timed_tan, lo_tan, up_tan = regroup(tangent_seed, lo_mask, up_mask, derivative, rotation)
    next_tan, previous_tangent = cycle_faces(lo_tan, up_tan)
    timed_adj, lo_adj, up_adj = regroup(negated, lo_mask, up_mask, derivative, rotation)
    next_adj, prev_adj = cycle_faces(-lo_scale * lo_adj, -up_scale * up_adj)
    shifted = jnp.pad(tangent_seed[..., :-1], ((0, 0), (0, 0), (0, 0), (1, 0)))
    applied = (
        block_apply(jacobian, tangent_seed) - upwind[:, None, None, :] * shifted + OMEGA * timed_tan
    )
    applied = (
        applied
        - face_spread(up_scale * next_tan, up_mask)
        - face_spread(lo_scale * previous_tangent, lo_mask)
    )
    tangent_out = block_apply(precond, applied)
    shifted = jnp.pad(
        (upwind[:, None, None, :] * dual_field)[..., 1:], ((0, 0), (0, 0), (0, 0), (0, 1))
    )
    adjoint_out = block_apply_t(jacobian, dual_field) - shifted + OMEGA * timed_adj
    adjoint_out = adjoint_out - face_spread(prev_adj, lo_mask) - face_spread(next_adj, up_mask)
    return (tangent_out, adjoint_out)


def solution(mesh):
    in_specs = (
        P("blade", None, "inst", None),
        P("blade", None, "inst", None),
        P("blade", "inst", None, None),
        P("blade", "inst", None, None),
        P("blade", None),
        P("blade", None),
        P("blade", None),
        P(),
        P(),
        P(),
    )
    out_specs = (P("blade", None, "inst", None), P("blade", None, "inst", None))
    return jax.shard_map(
        on_device, mesh=mesh, in_specs=in_specs, out_specs=out_specs, check_vma=False
    )
```

profile of v0, /device:TPU:1, one launch (start us, length us, event | category | flops | bytes accessed | tf_op | source)
XLA Modules:
  0.0 108.2 jit_solution(11999192427864549714)
XLA Ops:
  2.5 1.8 %fusion.170 = (f32[1,5,12,1024]{3,2,1,0:T(8,128)S(1)}, f32[1,5,12,1024]{3,2,1,0:T(8,128)S(1)}, f32[1,5,12,1024]{3,2,1,0:T(8,128)}) fusion(f32[1,5,12,1024]{3,0,2,1:T(1,128)} %param.10, f32[1024]{0:T(1024)S(1)} %get-tuple-element.88, f32[1024]{0:T(1024)S(1)} %get-tuple-element.89), kind=kLoop, calls=%fused_computation.354 | loop fusion | flops 122880 | bytes 991232 | tf_op args[0]
  4.3 1.7 %copy.312 = f32[1,5,12,1024]{2,3,1,0:T(8,128)S(1)} copy(f32[1,5,12,1024]{3,2,1,0:T(8,128)} %get-tuple-element.77) | data formatting | bytes 491520 | tf_op jit(solution)/shard_map/mul | solution.py:80
  6.0 2.9 %reduce_sum.66 = f32[5,12,256]{1,2,0:T(8,128)} reduce(f32[5,12,256,4]{1,3,2,0:T(4,128)S(1)} %bitcast.467, f32[]{:T(128)} %constant.66.clone.1), dimensions={3}, to_apply=%region_3.4 | reduce | flops 46080 | bytes 307204 | tf_op jit(solution)/shard_map/reduce_sum | solution.py:81
  10.3 8.5 %all-gather.1 = f32[5,24,256]{2,0,1:T(8,128)S(1)} all-gather(f32[5,12,256]{2,0,1:T(8,128)S(1)} %copy.313), channel_id=3, replica_groups=mesh['blade'=256,'inst'=2] {'inst'}, dimensions={1}, use_global_device_ids=true | all-gather | bytes 184320 | tf_op jit(solution)/shard_map/all_gather | solution.py:99
  18.8 1.7 %multiply_reduce_fusion.2 = (f32[24,24]{1,0:T(8,128)}, f32[24,24]{1,0:T(8,128)S(1)}) fusion(s32[24,24]{1,0:T(8,128)S(1)} %iota_subtract_fusion, s32[11]{0:T(128)S(1)} %get-tuple-element.90, f32[11]{0:T(128)S(1)} %get-tuple-element.91, f32[11]{0:T(128)S(1)} %convert_multiply_fusion.75), kind=kLoop, calls=%fused_computation.31 | loop fusion | flops 93888 | bytes 7044 | tf_op jit(solution)/shard_map/reduce_sum | solution.py:28
  21.5 1.9 %collective-permute-start.1 = (f32[1,5,12,256]{3,2,1,0:T(8,128)}, f32[1,5,12,256]{3,2,1,0:T(8,128)}, u32[]{:S(2)}, u32[]{:S(2)}) collective-permute-start(f32[1,5,12,256]{3,2,1,0:T(8,128)} %convolution_bitcast_fusion.2), channel_id=1, source_target_pairs={{510,0},{0,2},{2,4},{4,6},{6,8},{8,10},{10,12},{12,14},{14,16},{16... | collective-permute-start | bytes 184328 | tf_op jit(solution)/shard_map/ppermute | solution.py:14
  24.2 2.9 %reduce_sum.63 = f32[5,12,256]{1,2,0:T(8,128)} reduce(f32[5,12,256,4]{1,3,2,0:T(4,128)S(1)} %bitcast.466, f32[]{:T(128)} %constant.66.clone.1), dimensions={3}, to_apply=%region_1.2 | reduce | flops 46080 | bytes 307204 | tf_op jit(solution)/shard_map/reduce_sum | solution.py:81
  28.5 1.9 %all-gather = f32[5,24,256]{2,0,1:T(8,128)S(1)} all-gather(f32[5,12,256]{2,0,1:T(8,128)S(1)} %copy.307), channel_id=2, replica_groups=mesh['blade'=256,'inst'=2] {'inst'}, dimensions={1}, use_global_device_ids=true | all-gather | bytes 184320 | tf_op jit(solution)/shard_map/all_gather | solution.py:98
  31.4 10.7 %collective-permute-start = (f32[1,5,12,256]{3,2,1,0:T(8,128)}, f32[1,5,12,256]{3,2,1,0:T(8,128)}, u32[]{:S(2)}, u32[]{:S(2)}) collective-permute-start(f32[1,5,12,256]{3,2,1,0:T(8,128)} %convolution_bitcast_fusion.3), channel_id=1, source_target_pairs={{2,0},{4,2},{6,4},{8,6},{10,8},{12,10},{14,12},{16,14},{18,16},{20... | collective-permute-start | bytes 184328 | tf_op jit(solution)/shard_map/ppermute | solution.py:14
  42.1 2.1 %fusion.168 = (bf16[1,12,1,1024]{3,2,1,0:T(2,128)(2,1)S(1)}, bf16[1,12,1,1024]{3,2,1,0:T(2,128)(2,1)S(1)}, bf16[1,12,1,1024]{3,2,1,0:T(2,128)(2,1)S(1)}, bf16[1,...) fusion(bf16[1,12,25,1024]{3,2,1,0:T(8,128)(2,1)} %param.12), kind=kLoop, calls=%fused_computation.352 | loop fusion | bytes 294912 | tf_op jit(solution)/shard_map/slice | solution.py:42
  44.1 4.7 %fusion.167 = (bf16[1,12,1,1024]{3,2,1,0:T(2,128)(2,1)}, bf16[1,12,1,1024]{3,2,1,0:T(2,128)(2,1)}, bf16[1,12,1,1024]{3,2,1,0:T(2,128)(2,1)}, bf16[1,12,1,1024]{3...) fusion(bf16[1,12,25,1024]{3,2,1,0:T(8,128)(2,1)} %param.12), kind=kLoop, calls=%fused_computation.351 | loop fusion | bytes 933888 | tf_op jit(solution)/shard_map/slice | solution.py:46
  55.3 2.4 %all-gather.3 = f32[5,24,256]{2,0,1:T(8,128)S(1)} all-gather(f32[5,12,256]{2,0,1:T(8,128)S(1)} %copy.368), channel_id=5, replica_groups=mesh['blade'=256,'inst'=2] {'inst'}, dimensions={1}, use_global_device_ids=true | all-gather | bytes 184320 | tf_op jit(solution)/shard_map/all_gather | solution.py:98
  58.6 3.6 %collective-permute-start.3 = (f32[1,5,12,256]{3,2,1,0:T(8,128)}, f32[1,5,12,256]{3,2,1,0:T(8,128)}, u32[]{:S(2)}, u32[]{:S(2)}) collective-permute-start(f32[1,5,12,256]{3,2,1,0:T(8,128)} %fusion.11), channel_id=1, source_target_pairs={{2,0},{4,2},{6,4},{8,6},{10,8},{12,10},{14,12},{16,14},{18,16},{20... | collective-permute-start | bytes 184328 | tf_op jit(solution)/shard_map/ppermute | solution.py:14
  62.3 2.4 %all-gather.2 = f32[5,24,256]{2,0,1:T(8,128)S(1)} all-gather(f32[5,12,256]{2,0,1:T(8,128)S(1)} %copy.361), channel_id=4, replica_groups=mesh['blade'=256,'inst'=2] {'inst'}, dimensions={1}, use_global_device_ids=true | all-gather | bytes 184320 | tf_op jit(solution)/shard_map/all_gather | solution.py:99
  65.6 2.0 %collective-permute-start.2 = (f32[1,5,12,256]{3,2,1,0:T(8,128)}, f32[1,5,12,256]{3,2,1,0:T(8,128)}, u32[]{:S(2)}, u32[]{:S(2)}) collective-permute-start(f32[1,5,12,256]{3,2,1,0:T(8,128)} %fusion.9), channel_id=1, source_target_pairs={{510,0},{0,2},{2,4},{4,6},{6,8},{8,10},{10,12},{12,14},{14,16},{16... | collective-permute-start | bytes 184328 | tf_op jit(solution)/shard_map/ppermute | solution.py:14
  67.7 2.2 %all_gather.18 = f32[1,5,24,1024]{3,0,1,2:T(1,128)S(1)} all-gather(f32[1,5,12,1024]{3,0,1,2:T(1,128)S(1)} %copy.303), channel_id=1, replica_groups=mesh['blade'=256,'inst'=2] {'inst'}, dimensions={2}, use_global_device_ids=true | all-gather | bytes 737280 | tf_op jit(solution)/shard_map/all_gather | solution.py:97
  77.0 2.5 %all_gather.21 = f32[1,5,24,1024]{3,0,1,2:T(1,128)} all-gather(f32[1,5,12,1024]{3,0,1,2:T(1,128)S(1)} %copy.347), channel_id=1, replica_groups=mesh['blade'=256,'inst'=2] {'inst'}, dimensions={2}, use_global_device_ids=true | all-gather | bytes 737280 | tf_op jit(solution)/shard_map/all_gather | solution.py:97
  87.7 1.5 %broadcast_in_dim.21 = f32[5,12,256,4]{1,3,2,0:T(4,128)S(1)} broadcast(f32[5,12,256]{1,2,0:T(8,128)} %copy.309), dimensions={0,1,2} | broadcast | bytes 307200 | tf_op jit(solution)/shard_map/broadcast_in_dim | solution.py:85
  91.0 1.9 %fusion.4 = f32[1,5,12,1024]{3,2,1,0:T(8,128)S(1)} fusion(f32[1,5,24,1024]{3,0,1,2:T(1,128)S(1)} %all_gather.18, f32[1,5,12,1024]{3,2,1,0:T(8,128)} %copy.317, f32[1,5,12,1024]{3,2,1,0:T(8,128)} %copy.310, f32[1,5,12,1024]{3,2,1,0:T(8,128)} %copy-done.5, f32[1,5,12,1023]{3,2,1,0:T(8,128)S(1)} %bitcast.465, f32[1024]{0:T(1024)S(1)} %get-tuple-element.89, ...), kind=kOutput, calls=%fused_computation.6 | convolution fusion | flops 18186528 | bytes 1987476 | tf_op jit(solution)/shard_map/ts,pvsc->pvtc/dot_general | solution.py:67
  95.2 2.0 %copy.370 = f32[5,12,256]{1,2,0:T(8,128)} copy(f32[5,12,256]{2,1,0:T(8,128)} %bitcast.136) | data formatting | bytes 122880 | tf_op jit(solution)/shard_map/ppermute | solution.py:14
  97.3 1.5 %broadcast_in_dim.52 = f32[5,12,256,4]{1,3,2,0:T(4,128)S(1)} broadcast(f32[5,12,256]{1,2,0:T(8,128)} %copy.370), dimensions={0,1,2} | broadcast | bytes 307200 | tf_op jit(solution)/shard_map/broadcast_in_dim | solution.py:85
  100.3 2.0 %copy.364 = f32[5,12,256]{1,2,0:T(8,128)} copy(f32[5,12,256]{2,1,0:T(8,128)} %bitcast.132) | data formatting | bytes 122880 | tf_op jit(solution)/shard_map/ppermute | solution.py:14
  102.3 1.6 %broadcast_in_dim.50 = f32[5,12,256,4]{1,3,2,0:T(4,128)S(1)} broadcast(f32[5,12,256]{1,2,0:T(8,128)} %copy.364), dimensions={0,1,2} | broadcast | bytes 307200 | tf_op jit(solution)/shard_map/broadcast_in_dim | solution.py:85
  105.5 1.7 %fusion.7 = f32[1,5,12,1024]{3,2,1,0:T(8,128)S(1)} fusion(f32[1,5,24,1024]{3,0,1,2:T(1,128)S(1)} %copy-done, f32[1,5,12,1024]{3,2,1,0:T(8,128)} %copy.371, f32[1,5,12,1024]{3,2,1,0:T(8,128)} %copy.365, f32[1,5,12,1024]{3,2,1,0:T(8,128)} %copy-done.4, f32[1,5,12,1023]{3,2,1,0:T(8,128)S(1)} %copy-done.2, f32[1024]{0:T(1024)S(1)} %get-tuple-element.89, ...), kind=kOutput, calls=%fused_computation.9 | convolution fusion | flops 18125088 | bytes 1826820 | tf_op jit(solution)/shard_map/ts,pvsc->pvtc/dot_general | solution.py:67
  (227 shorter events, 38.1 us)
Async XLA Ops:
  6.0 12.8 %copy-start.70 = (s32[11]{0:T(128)S(1)}, s32[11]{0:T(128)}, u32[]{:S(2)}) copy-start(s32[11]{0:T(128)} %param.19) | copy-start | bytes 136
  21.5 59.1 %collective-permute-start.1 = (f32[1,5,12,256]{3,2,1,0:T(8,128)}, f32[1,5,12,256]{3,2,1,0:T(8,128)}, u32[]{:S(2)}, u32[]{:S(2)}) collective-permute-start(f32[1,5,12,256]{3,2,1,0:T(8,128)} %convolution_bitcast_fusion.2), channel_id=1, source_target_pairs={{510,0},{0,2},{2,4},{4,6},{6,8},{8,10},{10,12},{12,14},{14,16},{16... | collective-permute-start | bytes 184328 | tf_op jit(solution)/shard_map/ppermute | solution.py:14
  27.0 21.8 %copy-start.1 = (bf16[1,12,25,1024]{3,2,1,0:T(8,128)(2,1)S(1)}, bf16[1,12,25,1024]{3,2,1,0:T(8,128)(2,1)}, u32[]{:S(2)}) copy-start(bf16[1,12,25,1024]{3,2,1,0:T(8,128)(2,1)} %param.13) | copy-start | bytes 1843204
  31.4 19.2 %copy-start.63 = (f32[1,5,12,1024]{3,0,2,1:T(1,128)S(1)}, f32[1,5,12,1024]{3,0,2,1:T(1,128)}, u32[]{:S(2)}) copy-start(f32[1,5,12,1024]{3,0,2,1:T(1,128)} %param.11) | copy-start | bytes 737284
  31.4 54.3 %collective-permute-start = (f32[1,5,12,256]{3,2,1,0:T(8,128)}, f32[1,5,12,256]{3,2,1,0:T(8,128)}, u32[]{:S(2)}, u32[]{:S(2)}) collective-permute-start(f32[1,5,12,256]{3,2,1,0:T(8,128)} %convolution_bitcast_fusion.3), channel_id=1, source_target_pairs={{2,0},{4,2},{6,4},{8,6},{10,8},{12,10},{14,12},{16,14},{18,16},{20... | collective-permute-start | bytes 184328 | tf_op jit(solution)/shard_map/ppermute | solution.py:14
  53.5 11.1 %copy-start.69 = (f32[1,256]{1,0:T(1,128)S(1)}, f32[1,256]{1,0:T(1,128)}, u32[]{:S(2)}) copy-start(f32[1,256]{1,0:T(1,128)} %param.15) | copy-start | bytes 3076
  53.5 14.1 %copy-start.3 = (f32[1,5,12,1024]{3,0,2,1:T(1,128)S(1)}, f32[1,5,12,1024]{3,0,2,1:T(1,128)}, u32[]{:S(2)}) copy-start(f32[1,5,12,1024]{3,0,2,1:T(1,128)} %param.10) | copy-start | bytes 737284
  54.4 16.9 %copy-start.50 = (bf16[1,12,1,1024]{3,2,1,0:T(2,128)(2,1)S(1)}, bf16[1,12,1,1024]{3,2,1,0:T(2,128)(2,1)}, u32[]{:S(2)}) copy-start(bf16[1,12,1,1024]{3,2,1,0:T(2,128)(2,1)} %get-tuple-element.60) | copy-start | bytes 73732
  54.4 16.9 %copy-start.54 = (bf16[1,12,1,1024]{3,2,1,0:T(2,128)(2,1)S(1)}, bf16[1,12,1,1024]{3,2,1,0:T(2,128)(2,1)}, u32[]{:S(2)}) copy-start(bf16[1,12,1,1024]{3,2,1,0:T(2,128)(2,1)} %get-tuple-element.61) | copy-start | bytes 73732
  54.6 17.6 %copy-start.49 = (bf16[1,12,1,1024]{3,2,1,0:T(2,128)(2,1)S(1)}, bf16[1,12,1,1024]{3,2,1,0:T(2,128)(2,1)}, u32[]{:S(2)}) copy-start(bf16[1,12,1,1024]{3,2,1,0:T(2,128)(2,1)} %get-tuple-element.55) | copy-start | bytes 73732
  54.6 17.6 %copy-start.53 = (bf16[1,12,1,1024]{3,2,1,0:T(2,128)(2,1)S(1)}, bf16[1,12,1,1024]{3,2,1,0:T(2,128)(2,1)}, u32[]{:S(2)}) copy-start(bf16[1,12,1,1024]{3,2,1,0:T(2,128)(2,1)} %get-tuple-element.56) | copy-start | bytes 73732
  54.7 17.6 %copy-start.60 = (bf16[1,12,1,1024]{3,2,1,0:T(2,128)(2,1)S(1)}, bf16[1,12,1,1024]{3,2,1,0:T(2,128)(2,1)}, u32[]{:S(2)}) copy-start(bf16[1,12,1,1024]{3,2,1,0:T(2,128)(2,1)} %get-tuple-element.57) | copy-start | bytes 73732
  54.9 18.2 %copy-start.56 = (bf16[1,12,1,1024]{3,2,1,0:T(2,128)(2,1)S(1)}, bf16[1,12,1,1024]{3,2,1,0:T(2,128)(2,1)}, u32[]{:S(2)}) copy-start(bf16[1,12,1,1024]{3,2,1,0:T(2,128)(2,1)} %get-tuple-element.48) | copy-start | bytes 73732
  55.3 18.7 %copy-start.48 = (bf16[1,12,1,1024]{3,2,1,0:T(2,128)(2,1)S(1)}, bf16[1,12,1,1024]{3,2,1,0:T(2,128)(2,1)}, u32[]{:S(2)}) copy-start(bf16[1,12,1,1024]{3,2,1,0:T(2,128)(2,1)} %get-tuple-element.50) | copy-start | bytes 73732
  55.3 18.7 %copy-start.52 = (bf16[1,12,1,1024]{3,2,1,0:T(2,128)(2,1)S(1)}, bf16[1,12,1,1024]{3,2,1,0:T(2,128)(2,1)}, u32[]{:S(2)}) copy-start(bf16[1,12,1,1024]{3,2,1,0:T(2,128)(2,1)} %get-tuple-element.51) | copy-start | bytes 73732
  55.3 18.7 %copy-start.59 = (bf16[1,12,1,1024]{3,2,1,0:T(2,128)(2,1)S(1)}, bf16[1,12,1,1024]{3,2,1,0:T(2,128)(2,1)}, u32[]{:S(2)}) copy-start(bf16[1,12,1,1024]{3,2,1,0:T(2,128)(2,1)} %get-tuple-element.52) | copy-start | bytes 73732
  58.6 36.7 %collective-permute-start.3 = (f32[1,5,12,256]{3,2,1,0:T(8,128)}, f32[1,5,12,256]{3,2,1,0:T(8,128)}, u32[]{:S(2)}, u32[]{:S(2)}) collective-permute-start(f32[1,5,12,256]{3,2,1,0:T(8,128)} %fusion.11), channel_id=1, source_target_pairs={{2,0},{4,2},{6,4},{8,6},{10,8},{12,10},{14,12},{16,14},{18,16},{20... | collective-permute-start | bytes 184328 | tf_op jit(solution)/shard_map/ppermute | solution.py:14
  62.3 12.7 %copy-start.55 = (bf16[1,12,1,1024]{3,2,1,0:T(2,128)(2,1)S(1)}, bf16[1,12,1,1024]{3,2,1,0:T(2,128)(2,1)}, u32[]{:S(2)}) copy-start(bf16[1,12,1,1024]{3,2,1,0:T(2,128)(2,1)} %get-tuple-element.47) | copy-start | bytes 73732
  65.6 10.3 %copy-start.47 = (bf16[1,12,1,1024]{3,2,1,0:T(2,128)(2,1)S(1)}, bf16[1,12,1,1024]{3,2,1,0:T(2,128)(2,1)}, u32[]{:S(2)}) copy-start(bf16[1,12,1,1024]{3,2,1,0:T(2,128)(2,1)} %get-tuple-element.45) | copy-start | bytes 73732
  65.6 10.3 %copy-start.51 = (bf16[1,12,1,1024]{3,2,1,0:T(2,128)(2,1)S(1)}, bf16[1,12,1,1024]{3,2,1,0:T(2,128)(2,1)}, u32[]{:S(2)}) copy-start(bf16[1,12,1,1024]{3,2,1,0:T(2,128)(2,1)} %get-tuple-element.46) | copy-start | bytes 73732
  65.6 10.3 %copy-start.58 = (bf16[1,12,1,1024]{3,2,1,0:T(2,128)(2,1)S(1)}, bf16[1,12,1,1024]{3,2,1,0:T(2,128)(2,1)}, u32[]{:S(2)}) copy-start(bf16[1,12,1,1024]{3,2,1,0:T(2,128)(2,1)} %copy-done.57) | copy-start | bytes 73732
  65.6 34.7 %collective-permute-start.2 = (f32[1,5,12,256]{3,2,1,0:T(8,128)}, f32[1,5,12,256]{3,2,1,0:T(8,128)}, u32[]{:S(2)}, u32[]{:S(2)}) collective-permute-start(f32[1,5,12,256]{3,2,1,0:T(8,128)} %fusion.9), channel_id=1, source_target_pairs={{510,0},{0,2},{2,4},{4,6},{6,8},{8,10},{10,12},{12,14},{14,16},{16... | collective-permute-start | bytes 184328 | tf_op jit(solution)/shard_map/ppermute | solution.py:14
  74.1 5.4 %copy-start.66 = (f32[1,1024]{1,0:T(1,128)S(1)}, f32[1,1024]{1,0:T(1,128)}, u32[]{:S(2)}) copy-start(f32[1,1024]{1,0:T(1,128)} %param.14) | copy-start | bytes 12292
  75.0 5.6 %copy-start.68 = (f32[1,256]{1,0:T(1,128)S(1)}, f32[1,256]{1,0:T(1,128)}, u32[]{:S(2)}) copy-start(f32[1,256]{1,0:T(1,128)} %param.16) | copy-start | bytes 3076
  (51 other events, 151.4 us)
where the time goes:
time: 110 us; the launch traced here: 108 us
  local copies, waits for them, and re-layouts  39.6 us (36%)
  other arithmetic  21.2 us (19%)
  blocking collectives  19.8 us (18%)
  starting transfers between devices  18.3 us (17%)
  matrix products  7.35 us (7%)
  between operations  1.95 us (2%)
    ppermute x4, starting transfers between devices, passed_along(): return lax.ppermute(block, axis, route)  18.3 us
    broadcast_in_dim x8, local copies, waits for them, and re-layouts, face_spread(): return jnp.repeat(values, 4, axis=-1) * mask  12.2 us
    all_gather x2, blocking collectives, regroup(): lax.all_gather(up_face, 'inst', axis=2, tiled=True)  10.8 us
    unnamed x13, other arithmetic  8.42 us
    dot_general x6, matrix products, instance_mix(): jnp.einsum('ts,pvsc->pvtc', matrix, vector, precision=lax.Precision.HIGHEST)  7.35 us
    reduce_sum x3, other arithmetic, face_pick(): return jnp.sum(picked, axis=-1)  6.04 us
    slice x2, local copies, waits for them, and re-layouts, block_apply(): blocks[:, :, row_index * variables + column_index, :]  5.68 us
    all_gather x2, blocking collectives, regroup(): lax.all_gather(vector, 'inst', axis=2, tiled=True)  4.67 us
  transfers between devices with their start and end apart: 4, of which 0 were waited for; matrix products, arithmetic and copies ran while one was open for 44% of the time, Pallas kernels for 0%

commit v1 on v0

--- a/solution.py
+++ b/solution.py
@@ -6,6 +6,11 @@
 SNAPSHOT_COUNT = 24
 NH = 11
 OMEGA = 0.15
+
+
+def exchange_gather(x, axis, dim):
+    stack = jnp.stack([x] * lax.axis_size(axis))
+    return jnp.concatenate(lax.all_to_all(stack, axis, 0, 0), axis=dim)
 
 
 def passed_along(block, axis, distance):
@@ -95,7 +100,7 @@
     own_rot_t = lax.dynamic_slice_in_dim(rotation.T, first_row, own_count, 0)
     return (
         instance_mix(own_deriv, lax.all_gather(vector, "inst", axis=2, tiled=True)),
-        instance_mix(own_rot, lax.all_gather(lo_face, "inst", axis=2, tiled=True)),
+        instance_mix(own_rot, exchange_gather(lo_face, "inst", 2)),
         instance_mix(own_rot_t, lax.all_gather(up_face, "inst", axis=2, tiled=True)),
     )
 

time: 110 us -> 104 us (0.945); the launches traced: 108 us -> 103 us
  local copies, waits for them, and re-layouts: 39.6 us -> 34.2 us
  blocking collectives: 19.8 us -> 23.6 us
  other arithmetic: 21.2 us -> 17.8 us
    all_to_all x0 -> x2, blocking collectives: none -> 7.94 us  [exchange_gather(): return jnp.concatenate(lax.all_to_all(stack, axis, 0, 0), axis=dim)]
    unnamed x13, other arithmetic: 8.42 us -> 3.55 us
    all_gather x2 -> x0, blocking collectives: 4.31 us -> none  [regroup(): lax.all_gather(lo_face, 'inst', axis=2, tiled=True)]
    slice x2, local copies, waits for them, and re-layouts: 5.68 us -> 2.67 us  [block_apply(): blocks[:, :, row_index * variables + column_index, :]]
    reduce_sum x4 -> x2, local copies, waits for them, and re-layouts: 3 us -> 1.46 us  [face_pick(): return jnp.sum(picked, axis=-1)]
    another operation x0 -> x2, other arithmetic: none -> 1.49 us  [exchange_gather(): stack = jnp.stack([x] * lax.axis_size(axis))]
    slice x2, local copies, waits for them, and re-layouts: 2.33 us -> 1.16 us  [block_apply(): summed = blocks[:, :, row_index * variables, :] * vector[:, 0]]
    unnamed x151 -> x194, local copies, waits for them, and re-layouts: 2.94 us -> 3.97 us
  transfers between devices with their start and end apart: 4 -> 4, of which waited for: 0 -> 0; matrix products, arithmetic and copies ran while one was open for 44% -> 37% of each run, Pallas kernels for 0% -> 0%
where the time goes in v1:
time: 104 us; the launch traced here: 103 us
  local copies, waits for them, and re-layouts  34.2 us (33%)
  blocking collectives  23.6 us (23%)
  starting transfers between devices  18.2 us (18%)
  other arithmetic  17.8 us (17%)
  matrix products  7.29 us (7%)
  between operations  2.23 us (2%)
    ppermute x4, starting transfers between devices, passed_along(): return lax.ppermute(block, axis, route)  18.2 us
    broadcast_in_dim x8, local copies, waits for them, and re-layouts, face_spread(): return jnp.repeat(values, 4, axis=-1) * mask  12.1 us
    all_gather x2, blocking collectives, regroup(): lax.all_gather(up_face, 'inst', axis=2, tiled=True)  10.8 us
    all_to_all x2, blocking collectives, exchange_gather(): return jnp.concatenate(lax.all_to_all(stack, axis, 0, 0), axis=dim)  7.94 us
    dot_general x6, matrix products, instance_mix(): jnp.einsum('ts,pvsc->pvtc', matrix, vector, precision=lax.Precision.HIGHEST)  7.29 us
    reduce_sum x3, other arithmetic, face_pick(): return jnp.sum(picked, axis=-1)  6 us
    all_gather x2, blocking collectives, regroup(): lax.all_gather(vector, 'inst', axis=2, tiled=True)  4.79 us
    ppermute x2, local copies, waits for them, and re-layouts, passed_along(): return lax.ppermute(block, axis, route)  4 us
  transfers between devices with their start and end apart: 4, of which 0 were waited for; matrix products, arithmetic and copies ran while one was open for 37% of the time, Pallas kernels for 0%

profile of v1, /device:TPU:1, one launch (start us, length us, event | category | flops | bytes accessed | tf_op | source)
XLA Modules:
  0.0 103.3 jit_solution(16436088580404145989)
XLA Ops:
  2.5 1.8 %fusion.168 = (f32[1,5,12,1024]{3,2,1,0:T(8,128)S(1)}, f32[1,5,12,1024]{3,2,1,0:T(8,128)S(1)}, f32[1,5,12,1024]{3,2,1,0:T(8,128)}) fusion(f32[1,5,12,1024]{3,0,2,1:T(1,128)} %param.10, f32[1024]{0:T(1024)S(1)} %get-tuple-element.90, f32[1024]{0:T(1024)S(1)} %get-tuple-element.91), kind=kLoop, calls=%fused_computation.354 | loop fusion | flops 122880 | bytes 991232 | tf_op args[0]
  4.3 1.7 %copy.420 = f32[1,5,12,1024]{2,3,1,0:T(8,128)S(1)} copy(f32[1,5,12,1024]{3,2,1,0:T(8,128)} %get-tuple-element.79) | data formatting | bytes 491520 | tf_op jit(solution)/shard_map/mul | solution.py:85
  6.0 2.8 %reduce_sum.61 = f32[5,12,256]{1,2,0:T(8,128)} reduce(f32[5,12,256,4]{1,3,2,0:T(4,128)S(1)} %bitcast.473, f32[]{:T(128)} %constant.66.clone.1), dimensions={3}, to_apply=%region_3.4 | reduce | flops 46080 | bytes 307204 | tf_op jit(solution)/shard_map/reduce_sum | solution.py:86
  10.3 8.5 %all-gather = f32[5,24,256]{2,0,1:T(8,128)S(1)} all-gather(f32[5,12,256]{2,0,1:T(8,128)S(1)} %copy.421), channel_id=2, replica_groups=mesh['blade'=256,'inst'=2] {'inst'}, dimensions={1}, use_global_device_ids=true | all-gather | bytes 184320 | tf_op jit(solution)/shard_map/all_gather | solution.py:104
  18.8 1.6 %multiply_reduce_fusion.2 = (f32[24,24]{1,0:T(8,128)}, f32[24,24]{1,0:T(8,128)S(1)}) fusion(s32[24,24]{1,0:T(8,128)S(1)} %iota_subtract_fusion, s32[11]{0:T(128)S(1)} %get-tuple-element.92, f32[11]{0:T(128)S(1)} %get-tuple-element.93, f32[11]{0:T(128)S(1)} %convert_multiply_fusion.75), kind=kLoop, calls=%fused_computation.33 | loop fusion | flops 93888 | bytes 7044 | tf_op jit(solution)/shard_map/reduce_sum | solution.py:33
  21.4 1.9 %collective-permute-start.1 = (f32[1,5,12,256]{3,2,1,0:T(8,128)}, f32[1,5,12,256]{3,2,1,0:T(8,128)}, u32[]{:S(2)}, u32[]{:S(2)}) collective-permute-start(f32[1,5,12,256]{3,2,1,0:T(8,128)} %convolution_bitcast_fusion.2), channel_id=1, source_target_pairs={{510,0},{0,2},{2,4},{4,6},{6,8},{8,10},{10,12},{12,14},{14,16},{16... | collective-permute-start | bytes 184328 | tf_op jit(solution)/shard_map/ppermute | solution.py:19
  24.1 2.8 %reduce_sum.59 = f32[5,12,256]{1,2,0:T(8,128)} reduce(f32[5,12,256,4]{1,3,2,0:T(4,128)S(1)} %bitcast.472, f32[]{:T(128)} %constant.66.clone.1), dimensions={3}, to_apply=%region_1.2 | reduce | flops 46080 | bytes 307204 | tf_op jit(solution)/shard_map/reduce_sum | solution.py:86
  28.8 3.8 %all_to_all.10 = f32[2,1,5,12,256]{4,1,3,2,0:T(1,128)S(1)} all-to-all(f32[2,1,5,12,256]{4,1,3,2,0:T(1,128)S(1)} %copy.415), channel_id=1, replica_groups=mesh['blade'=256,'inst'=2] {'inst'}, dimensions={0} | all-to-all | bytes 245760 | tf_op jit(solution)/shard_map/all_to_all | solution.py:13
  33.5 10.6 %collective-permute-start = (f32[1,5,12,256]{3,2,1,0:T(8,128)}, f32[1,5,12,256]{3,2,1,0:T(8,128)}, u32[]{:S(2)}, u32[]{:S(2)}) collective-permute-start(f32[1,5,12,256]{3,2,1,0:T(8,128)} %convolution_bitcast_fusion.3), channel_id=1, source_target_pairs={{2,0},{4,2},{6,4},{8,6},{10,8},{12,10},{14,12},{16,14},{18,16},{20... | collective-permute-start | bytes 184328 | tf_op jit(solution)/shard_map/ppermute | solution.py:19
  45.0 1.7 %fusion.165 = (bf16[1,12,1,1024]{3,2,1,0:T(2,128)(2,1)}, bf16[1,12,1,1024]{3,2,1,0:T(2,128)(2,1)}, bf16[1,12,1,1024]{3,2,1,0:T(2,128)(2,1)}, bf16[1,12,1,1024]{3...) fusion(bf16[1,12,25,1024]{3,2,1,0:T(8,128)(2,1)S(1)} %copy-done.1), kind=kLoop, calls=%fused_computation.351 | loop fusion | bytes 933888 | tf_op jit(solution)/shard_map/slice | solution.py:51
  53.4 4.1 %all_to_all.11 = f32[2,1,5,12,256]{4,1,3,2,0:T(1,128)S(1)} all-to-all(f32[2,1,5,12,256]{4,1,3,2,0:T(1,128)S(1)} %copy.476), channel_id=1, replica_groups=mesh['blade'=256,'inst'=2] {'inst'}, dimensions={0} | all-to-all | bytes 245760 | tf_op jit(solution)/shard_map/all_to_all | solution.py:13
  58.5 3.6 %collective-permute-start.3 = (f32[1,5,12,256]{3,2,1,0:T(8,128)}, f32[1,5,12,256]{3,2,1,0:T(8,128)}, u32[]{:S(2)}, u32[]{:S(2)}) collective-permute-start(f32[1,5,12,256]{3,2,1,0:T(8,128)} %fusion.11), channel_id=1, source_target_pairs={{2,0},{4,2},{6,4},{8,6},{10,8},{12,10},{14,12},{16,14},{18,16},{20... | collective-permute-start | bytes 184328 | tf_op jit(solution)/shard_map/ppermute | solution.py:19
  62.2 2.4 %all-gather.1 = f32[5,24,256]{2,0,1:T(8,128)S(1)} all-gather(f32[5,12,256]{2,0,1:T(8,128)S(1)} %copy.469), channel_id=3, replica_groups=mesh['blade'=256,'inst'=2] {'inst'}, dimensions={1}, use_global_device_ids=true | all-gather | bytes 184320 | tf_op jit(solution)/shard_map/all_gather | solution.py:104
  65.6 2.1 %collective-permute-start.2 = (f32[1,5,12,256]{3,2,1,0:T(8,128)}, f32[1,5,12,256]{3,2,1,0:T(8,128)}, u32[]{:S(2)}, u32[]{:S(2)}) collective-permute-start(f32[1,5,12,256]{3,2,1,0:T(8,128)} %fusion.9), channel_id=1, source_target_pairs={{510,0},{0,2},{2,4},{4,6},{6,8},{8,10},{10,12},{12,14},{14,16},{16... | collective-permute-start | bytes 184328 | tf_op jit(solution)/shard_map/ppermute | solution.py:19
  67.7 2.3 %all_gather.12 = f32[1,5,24,1024]{3,0,1,2:T(1,128)S(1)} all-gather(f32[1,5,12,1024]{3,0,1,2:T(1,128)S(1)} %copy.411), channel_id=1, replica_groups=mesh['blade'=256,'inst'=2] {'inst'}, dimensions={2}, use_global_device_ids=true | all-gather | bytes 737280 | tf_op jit(solution)/shard_map/all_gather | solution.py:102
  72.7 2.5 %all_gather.14 = f32[1,5,24,1024]{3,0,1,2:T(1,128)} all-gather(f32[1,5,12,1024]{3,0,1,2:T(1,128)S(1)} %copy.455), channel_id=1, replica_groups=mesh['blade'=256,'inst'=2] {'inst'}, dimensions={2}, use_global_device_ids=true | all-gather | bytes 737280 | tf_op jit(solution)/shard_map/all_gather | solution.py:102
  78.3 1.5 %broadcast_in_dim.48 = f32[5,12,256,4]{1,3,2,0:T(4,128)S(1)} broadcast(f32[5,12,256]{1,2,0:T(8,128)} %copy.424), dimensions={0,1,2} | broadcast | bytes 307200 | tf_op jit(solution)/shard_map/broadcast_in_dim | solution.py:90
  83.4 1.5 %broadcast_in_dim.21 = f32[5,12,256,4]{1,3,2,0:T(4,128)S(1)} broadcast(f32[5,12,256]{1,2,0:T(8,128)} %copy.417), dimensions={0,1,2} | broadcast | bytes 307200 | tf_op jit(solution)/shard_map/broadcast_in_dim | solution.py:90
  86.5 1.9 %fusion.4 = f32[1,5,12,1024]{3,2,1,0:T(8,128)S(1)} fusion(f32[1,5,24,1024]{3,0,1,2:T(1,128)S(1)} %all_gather.12, f32[1,5,12,1024]{3,2,1,0:T(8,128)} %copy.425, f32[1,5,12,1024]{3,2,1,0:T(8,128)} %copy.418, f32[1,5,12,1024]{3,2,1,0:T(8,128)} %copy-done.7, f32[1,5,12,1023]{3,2,1,0:T(8,128)S(1)} %bitcast.471, f32[1024]{0:T(1024)S(1)} %get-tuple-element.91, ...), kind=kOutput, calls=%fused_computation.8 | convolution fusion | flops 18186528 | bytes 1987476 | tf_op jit(solution)/shard_map/ts,pvsc->pvtc/dot_general | solution.py:72
  90.5 2.0 %copy.478 = f32[5,12,256]{1,2,0:T(8,128)} copy(f32[5,12,256]{2,1,0:T(8,128)} %bitcast.140) | data formatting | bytes 122880 | tf_op jit(solution)/shard_map/ppermute | solution.py:19
  92.5 1.5 %broadcast_in_dim.52 = f32[5,12,256,4]{1,3,2,0:T(4,128)S(1)} broadcast(f32[5,12,256]{1,2,0:T(8,128)} %copy.478), dimensions={0,1,2} | broadcast | bytes 307200 | tf_op jit(solution)/shard_map/broadcast_in_dim | solution.py:90
  95.5 2.0 %copy.472 = f32[5,12,256]{1,2,0:T(8,128)} copy(f32[5,12,256]{2,1,0:T(8,128)} %bitcast.134) | data formatting | bytes 122880 | tf_op jit(solution)/shard_map/ppermute | solution.py:19
  97.5 1.5 %broadcast_in_dim.50 = f32[5,12,256,4]{1,3,2,0:T(4,128)S(1)} broadcast(f32[5,12,256]{1,2,0:T(8,128)} %copy.472), dimensions={0,1,2} | broadcast | bytes 307200 | tf_op jit(solution)/shard_map/broadcast_in_dim | solution.py:90
  100.6 1.7 %fusion.7 = f32[1,5,12,1024]{3,2,1,0:T(8,128)S(1)} fusion(f32[1,5,24,1024]{3,0,1,2:T(1,128)S(1)} %copy-done, f32[1,5,12,1024]{3,2,1,0:T(8,128)} %copy.479, f32[1,5,12,1024]{3,2,1,0:T(8,128)} %copy.473, f32[1,5,12,1024]{3,2,1,0:T(8,128)} %copy-done.6, f32[1,5,12,1023]{3,2,1,0:T(8,128)S(1)} %copy-done.3, f32[1024]{0:T(1024)S(1)} %get-tuple-element.91, ...), kind=kOutput, calls=%fused_computation.11 | convolution fusion | flops 18125088 | bytes 1826820 | tf_op jit(solution)/shard_map/ts,pvsc->pvtc/dot_general | solution.py:72
  (276 shorter events, 33.0 us)
Async XLA Ops:
  6.0 12.8 %copy-start.91 = (s32[11]{0:T(128)S(1)}, s32[11]{0:T(128)}, u32[]{:S(2)}) copy-start(s32[11]{0:T(128)} %param.19) | copy-start | bytes 136
  21.4 54.9 %collective-permute-start.1 = (f32[1,5,12,256]{3,2,1,0:T(8,128)}, f32[1,5,12,256]{3,2,1,0:T(8,128)}, u32[]{:S(2)}, u32[]{:S(2)}) collective-permute-start(f32[1,5,12,256]{3,2,1,0:T(8,128)} %convolution_bitcast_fusion.2), channel_id=1, source_target_pairs={{510,0},{0,2},{2,4},{4,6},{6,8},{8,10},{10,12},{12,14},{14,16},{16... | collective-permute-start | bytes 184328 | tf_op jit(solution)/shard_map/ppermute | solution.py:19
  28.4 15.7 %copy-start.1 = (bf16[1,12,25,1024]{3,2,1,0:T(8,128)(2,1)S(1)}, bf16[1,12,25,1024]{3,2,1,0:T(8,128)(2,1)}, u32[]{:S(2)}) copy-start(bf16[1,12,25,1024]{3,2,1,0:T(8,128)(2,1)} %param.12) | copy-start | bytes 1843204
  32.6 14.0 %copy-start.2 = (bf16[1,12,25,1024]{3,2,1,0:T(8,128)(2,1)S(1)}, bf16[1,12,25,1024]{3,2,1,0:T(8,128)(2,1)}, u32[]{:S(2)}) copy-start(bf16[1,12,25,1024]{3,2,1,0:T(8,128)(2,1)} %param.13) | copy-start | bytes 1843204
  33.5 47.9 %collective-permute-start = (f32[1,5,12,256]{3,2,1,0:T(8,128)}, f32[1,5,12,256]{3,2,1,0:T(8,128)}, u32[]{:S(2)}, u32[]{:S(2)}) collective-permute-start(f32[1,5,12,256]{3,2,1,0:T(8,128)} %convolution_bitcast_fusion.3), channel_id=1, source_target_pairs={{2,0},{4,2},{6,4},{8,6},{10,8},{12,10},{14,12},{16,14},{18,16},{20... | collective-permute-start | bytes 184328 | tf_op jit(solution)/shard_map/ppermute | solution.py:19
  53.0 11.6 %copy-start.90 = (f32[1,256]{1,0:T(1,128)S(1)}, f32[1,256]{1,0:T(1,128)}, u32[]{:S(2)}) copy-start(f32[1,256]{1,0:T(1,128)} %param.15) | copy-start | bytes 3076
  53.0 14.6 %copy-start.4 = (f32[1,5,12,1024]{3,0,2,1:T(1,128)S(1)}, f32[1,5,12,1024]{3,0,2,1:T(1,128)}, u32[]{:S(2)}) copy-start(f32[1,5,12,1024]{3,0,2,1:T(1,128)} %param.10) | copy-start | bytes 737284
  57.6 12.5 %copy-start.86 = (f32[24,24]{1,0:T(8,128)S(1)}, f32[24,24]{1,0:T(8,128)}, u32[]{:S(2)}) copy-start(f32[24,24]{1,0:T(8,128)} %get-tuple-element.14) | copy-start | bytes 6916
  57.6 13.1 %copy-start.16 = (bf16[1,12,1,1024]{3,2,1,0:T(2,128)(2,1)S(1)}, bf16[1,12,1,1024]{3,2,1,0:T(2,128)(2,1)}, u32[]{:S(2)}) copy-start(bf16[1,12,1,1024]{3,2,1,0:T(2,128)(2,1)} %get-tuple-element.67) | copy-start | bytes 73732
  57.6 13.1 %copy-start.17 = (bf16[1,12,1,1024]{3,2,1,0:T(2,128)(2,1)S(1)}, bf16[1,12,1,1024]{3,2,1,0:T(2,128)(2,1)}, u32[]{:S(2)}) copy-start(bf16[1,12,1,1024]{3,2,1,0:T(2,128)(2,1)} %get-tuple-element.68) | copy-start | bytes 73732
  57.6 13.1 %copy-start.18 = (bf16[1,12,1,1024]{3,2,1,0:T(2,128)(2,1)S(1)}, bf16[1,12,1,1024]{3,2,1,0:T(2,128)(2,1)}, u32[]{:S(2)}) copy-start(bf16[1,12,1,1024]{3,2,1,0:T(2,128)(2,1)} %get-tuple-element.69) | copy-start | bytes 73732
  57.6 13.1 %copy-start.19 = (bf16[1,12,1,1024]{3,2,1,0:T(2,128)(2,1)S(1)}, bf16[1,12,1,1024]{3,2,1,0:T(2,128)(2,1)}, u32[]{:S(2)}) copy-start(bf16[1,12,1,1024]{3,2,1,0:T(2,128)(2,1)} %get-tuple-element.70) | copy-start | bytes 73732
  57.6 13.1 %copy-start.23 = (bf16[1,12,1,1024]{3,2,1,0:T(2,128)(2,1)S(1)}, bf16[1,12,1,1024]{3,2,1,0:T(2,128)(2,1)}, u32[]{:S(2)}) copy-start(bf16[1,12,1,1024]{3,2,1,0:T(2,128)(2,1)} %copy-done.22) | copy-start | bytes 73732
  58.5 32.0 %collective-permute-start.3 = (f32[1,5,12,256]{3,2,1,0:T(8,128)}, f32[1,5,12,256]{3,2,1,0:T(8,128)}, u32[]{:S(2)}, u32[]{:S(2)}) collective-permute-start(f32[1,5,12,256]{3,2,1,0:T(8,128)} %fusion.11), channel_id=1, source_target_pairs={{2,0},{4,2},{6,4},{8,6},{10,8},{12,10},{14,12},{16,14},{18,16},{20... | collective-permute-start | bytes 184328 | tf_op jit(solution)/shard_map/ppermute | solution.py:19
  62.2 8.7 %copy-start.21 = (bf16[1,12,1,1024]{3,2,1,0:T(2,128)(2,1)S(1)}, bf16[1,12,1,1024]{3,2,1,0:T(2,128)(2,1)}, u32[]{:S(2)}) copy-start(bf16[1,12,1,1024]{3,2,1,0:T(2,128)(2,1)} %copy-done.20) | copy-start | bytes 73732
  62.2 8.7 %copy-start.65 = (bf16[1,12,1,1024]{3,2,1,0:T(2,128)(2,1)S(1)}, bf16[1,12,1,1024]{3,2,1,0:T(2,128)(2,1)}, u32[]{:S(2)}) copy-start(bf16[1,12,1,1024]{3,2,1,0:T(2,128)(2,1)} %get-tuple-element.62) | copy-start | bytes 73732
  62.2 8.7 %copy-start.69 = (bf16[1,12,1,1024]{3,2,1,0:T(2,128)(2,1)S(1)}, bf16[1,12,1,1024]{3,2,1,0:T(2,128)(2,1)}, u32[]{:S(2)}) copy-start(bf16[1,12,1,1024]{3,2,1,0:T(2,128)(2,1)} %get-tuple-element.63) | copy-start | bytes 73732
  62.2 8.7 %copy-start.76 = (bf16[1,12,1,1024]{3,2,1,0:T(2,128)(2,1)S(1)}, bf16[1,12,1,1024]{3,2,1,0:T(2,128)(2,1)}, u32[]{:S(2)}) copy-start(bf16[1,12,1,1024]{3,2,1,0:T(2,128)(2,1)} %get-tuple-element.64) | copy-start | bytes 73732
  62.2 8.7 %copy-start.81 = (bf16[1,12,1,1024]{3,2,1,0:T(2,128)(2,1)S(1)}, bf16[1,12,1,1024]{3,2,1,0:T(2,128)(2,1)}, u32[]{:S(2)}) copy-start(bf16[1,12,1,1024]{3,2,1,0:T(2,128)(2,1)} %get-tuple-element.65) | copy-start | bytes 73732
  65.6 5.4 %copy-start.68 = (bf16[1,12,1,1024]{3,2,1,0:T(2,128)(2,1)S(1)}, bf16[1,12,1,1024]{3,2,1,0:T(2,128)(2,1)}, u32[]{:S(2)}) copy-start(bf16[1,12,1,1024]{3,2,1,0:T(2,128)(2,1)} %get-tuple-element.58) | copy-start | bytes 73732
  65.6 5.4 %copy-start.75 = (bf16[1,12,1,1024]{3,2,1,0:T(2,128)(2,1)S(1)}, bf16[1,12,1,1024]{3,2,1,0:T(2,128)(2,1)}, u32[]{:S(2)}) copy-start(bf16[1,12,1,1024]{3,2,1,0:T(2,128)(2,1)} %get-tuple-element.59) | copy-start | bytes 73732
  65.6 5.4 %copy-start.80 = (bf16[1,12,1,1024]{3,2,1,0:T(2,128)(2,1)S(1)}, bf16[1,12,1,1024]{3,2,1,0:T(2,128)(2,1)}, u32[]{:S(2)}) copy-start(bf16[1,12,1,1024]{3,2,1,0:T(2,128)(2,1)} %get-tuple-element.60) | copy-start | bytes 73732
  65.6 5.4 %copy-start.83 = (bf16[1,12,1,1024]{3,2,1,0:T(2,128)(2,1)S(1)}, bf16[1,12,1,1024]{3,2,1,0:T(2,128)(2,1)}, u32[]{:S(2)}) copy-start(bf16[1,12,1,1024]{3,2,1,0:T(2,128)(2,1)} %copy-done.82) | copy-start | bytes 73732
  65.6 29.9 %collective-permute-start.2 = (f32[1,5,12,256]{3,2,1,0:T(8,128)}, f32[1,5,12,256]{3,2,1,0:T(8,128)}, u32[]{:S(2)}, u32[]{:S(2)}) collective-permute-start(f32[1,5,12,256]{3,2,1,0:T(8,128)} %fusion.9), channel_id=1, source_target_pairs={{510,0},{0,2},{2,4},{4,6},{6,8},{8,10},{10,12},{12,14},{14,16},{16... | collective-permute-start | bytes 184328 | tf_op jit(solution)/shard_map/ppermute | solution.py:19
  (72 other events, 134.0 us)
